TPU v7x, 32 devices: a whole 2x2x4 slice. The times are simulated.
32 devices in a mesh: batch: 8 (over z, x), owner: 4 (over y, core).
Axes of the slice: x: 2, y: 2, z: 4, core: 2. Of those that a mesh axis runs over, the one named last changes fastest.
Arguments:
- queries: bfloat16 [128, 32, 128], P(('batch', 'owner')), may hold values from -8 to 8
- pool: bfloat16 [32, 184, 128], P(('owner', 'batch')), may hold values from -20 to 20
- lengths: int32 [32], P('owner'), may hold values from 46 to 180, as said below
- candidates: int32 [128, 12], P('batch'), may hold values from 0 to 31, as said below
- owner_map: int32 [32], replicated, may hold values from 0 to 31, as said below
- teacher: float32 [128, 12], P(('batch', 'owner')), may hold values from -12 to 12
Outputs:
- query_grad: float32 [128, 32, 128], P(('batch', 'owner'))
- divergence: float32 [128], P(('batch', 'owner'))
Inputs may be any that keep to these rules, and one draw needn't show every extreme that they name: `lengths`: every owner group (pool rows k * 8 to (k + 1) * 8 - 1) holds a passage of exactly 180 tokens. `owner_map`: A permutation: each pool row belongs to one passage id. Each query names 12 different passages. The owner group of a passage p is owner_map[p] // 8. All queries of one batch index have the same number of candidates in each owner group: 6 in some of the groups, 3 in half, none in a quarter; which groups these are differs between batch indices.
All inputs are finite; a program needn't handle non-finite values.
Results may differ from a plain program's by a relative error of at most 0.0075.
Values may be sent and summed in bfloat16 or wider, within the bound.
No kernel may reach another device: no remote copies, remote signals or barrier semaphores. Data moves between devices by JAX's collectives and lax.ppermute only.
A program may use at most 64 MiB of HBM per device.

v0:
```python
import math
import jax
import jax.numpy as jnp
from jax import lax
from jax.sharding import PartitionSpec as P

CPO = 3
SHARPNESS = 20.0
STUDENT_GAIN = 2.0
LOSS_SCALE = 64.0
EPSILON = 1e-06


def unit_rows(values):
    widened = values.astype(jnp.float32)
    inv_norm = lax.rsqrt(jnp.sum(widened * widened, axis=-1, keepdims=True) + EPSILON)
    return (widened * inv_norm, inv_norm)


def token_terms(query_block, passages, length_block):
    similar = jnp.einsum(
        "bid,bktd->bkit", query_block, passages, preferred_element_type=jnp.float32
    )
    in_range = lax.broadcasted_iota(jnp.int32, similar.shape, 3) < length_block[:, :, None, None]
    exp_terms = jnp.where(in_range, jnp.exp(SHARPNESS * similar), 0.0)
    return (exp_terms, jnp.sum(exp_terms, axis=3))


def loss_terms(scores, teacher_rows):
    student = STUDENT_GAIN * scores
    log_student = student - jnp.log(jnp.sum(jnp.exp(student), axis=1, keepdims=True))
    log_target = teacher_rows - jnp.log(jnp.sum(jnp.exp(teacher_rows), axis=1, keepdims=True))
    target = jnp.exp(log_target)
    divergence = jnp.sum(target * (log_target - log_student), axis=1)
    score_grad = LOSS_SCALE * STUDENT_GAIN * (jnp.exp(log_student) - target)
    return (divergence, score_grad)


def local(queries, pool, lengths, candidates, owner_map, teacher):
    own_rows = queries.shape[0]
    all_rows = candidates.shape[0]
    tok_count = queries.shape[1]
    feature = queries.shape[2]
    slot_cap = 2 * CPO
    my_group = lax.axis_index("owner")
    unit_query, inv_norm = unit_rows(queries)
    sent_query = unit_query.astype(jnp.bfloat16)
    gathered = lax.all_gather(sent_query, "owner", axis=0, tiled=True)
    shard_unit = unit_rows(pool)[0].astype(jnp.bfloat16)
    cached = lax.all_gather(shard_unit, "batch", axis=0, tiled=True)
    group_rows = cached.shape[0]
    slot_ids = jnp.take(owner_map, candidates, axis=0)
    local_slot = slot_ids - my_group * group_rows
    is_local = (local_slot >= 0) & (local_slot < group_rows)
    order_rank = jnp.cumsum(is_local.astype(jnp.int32), axis=1) - 1
    slot_iota = lax.broadcasted_iota(jnp.int32, (1, 1, slot_cap), 2)
    matches = is_local[:, :, None] & (order_rank[:, :, None] == slot_iota)
    filled = jnp.any(matches, axis=1)
    pick_slot = jnp.sum(jnp.where(matches, local_slot[:, :, None], 0), axis=1)
    length_of = jnp.where(filled, jnp.take(lengths, pick_slot, axis=0), 1)

    def block_inputs(first_row, row_span):
        query_block = lax.dynamic_slice_in_dim(gathered, first_row, row_span, 0)
        pick_block = lax.dynamic_slice_in_dim(pick_slot, first_row, row_span, 0)
        length_block = lax.dynamic_slice_in_dim(length_of, first_row, row_span, 0)
        return (query_block, jnp.take(cached, pick_block, axis=0), length_block)

    stride = math.gcd(all_rows, 8)

    def forward(block_index):
        query_block, passages, length_block = block_inputs(block_index * stride, stride)
        totals = token_terms(query_block, passages, length_block)[1]
        ratio = totals / length_block[:, :, None].astype(jnp.float32)
        return jnp.sum(jnp.log(ratio), axis=2) / SHARPNESS

    slot_scores = lax.map(forward, jnp.arange(all_rows // stride)).reshape(all_rows, slot_cap)
    dense = jnp.sum(jnp.where(matches, slot_scores[:, None, :], 0.0), axis=2)
    own_scores = lax.psum_scatter(dense, "owner", scatter_dimension=0, tiled=True)
    divergence, grad_own = loss_terms(own_scores, teacher)
    grad_rows = lax.all_gather(grad_own, "owner", axis=0, tiled=True)
    slot_grads = jnp.sum(jnp.where(matches, grad_rows[:, :, None], 0.0), axis=1)
    groups = lax.axis_size("owner")
    inner = math.gcd(all_rows, 8)

    def one_block(block_index):
        first_row = 0 + block_index * inner
        query_block, passages, length_block = block_inputs(first_row, inner)
        grad_block = lax.dynamic_slice_in_dim(slot_grads, first_row, inner, 0)
        exp_terms, totals = token_terms(query_block, passages, length_block)
        weights = (exp_terms / totals[:, :, :, None]).astype(jnp.bfloat16)
        mixed = jnp.einsum("bkit,bktd->bkid", weights, passages, preferred_element_type=jnp.float32)
        return jnp.einsum("bk,bkid->bid", grad_block, mixed, precision=lax.Precision.HIGHEST)

    partials = (
        lax.map(one_block, jnp.arange(all_rows // inner))
        .reshape(all_rows, tok_count, feature)
        .reshape(groups, own_rows, tok_count, feature)
    )
    arrived = lax.all_to_all(partials, "owner", split_axis=0, concat_axis=0, tiled=True)
    unit_grad = jnp.sum(arrived, axis=0)
    radial = jnp.sum(unit_query * unit_grad, axis=-1, keepdims=True)
    query_grad = (unit_grad - unit_query * radial) * inv_norm
    return (query_grad, divergence)


def solution(mesh):
    in_specs = (
        P(("batch", "owner"), None, None),
        P(("owner", "batch"), None, None),
        P("owner"),
        P("batch", None),
        P(),
        P(("batch", "owner"), None),
    )
    out_specs = (P(("batch", "owner"), None, None), P(("batch", "owner")))
    return jax.shard_map(local, mesh=mesh, in_specs=in_specs, out_specs=out_specs, check_vma=False)
```

profile of v0, /device:TPU:0, one launch (start us, length us, event | category | flops | bytes accessed | tf_op | source)
XLA Modules:
  0.0 102.2 jit_solution(10071462860876659092)
XLA Ops:
  0.6 0.7 compare_select_fusion.2
  1.4 0.1 reshape.112
  1.5 1.6 %gather_fusion.2 = s32[192]{0:T(256)S(1)} fusion(s32[32]{0:T(128)S(1)} %copy-done, s32[1024]{0:T(1024)S(1)} %pad_clamp_fusion.3), kind=kCustom, calls=%fused_computation.2 | custom fusion | bytes 2304 | tf_op jit(solution)/shard_map/jit(_take)/gather | solution.py:52
  3.0 0.1 reshape.111
  3.2 0.2 reduce_window_sum.11
  3.3 0.2 fusion.37
  3.5 0.2 select_reduce_fusion.2
  3.7 0.1 copy.46
  3.8 0.1 copy.43
  3.9 0.1 reshape.120
  4.0 1.2 %gather_fusion.3 = s32[96]{0:T(128)S(1)} fusion(s32[8]{0:T(128)S(1)} %copy-done.1, s32[1024]{0:T(1024)S(1)} %pad_clamp_fusion.2), kind=kCustom, calls=%fused_computation.3 | custom fusion | bytes 1152 | tf_op jit(solution)/shard_map/jit(_take)/gather | solution.py:60
  5.3 0.1 reshape.119
  5.3 0.1 copy.44
  5.4 0.1 copy.45
  5.5 0.1 fusion.35
  5.6 0.1 fusion.32
  5.7 7.0 %all_gather.10 = bf16[16,32,128]{2,1,0:T(8,128)(2,1)} all-gather(bf16[4,32,128]{2,1,0:T(8,128)(2,1)S(1)} %fusion.32), channel_id=1, replica_groups=mesh['batch'=8,'owner'=4] {'owner'}, dimensions={0}, use_global_device_ids=true | all-gather | bytes 163840 | tf_op jit(solution)/shard_map/all_gather | solution.py:48
  12.7 0.1 fusion.29
  12.8 0.1 fusion.30
  12.9 31.8 %all_gather.9 = bf16[8,184,128]{2,1,0:T(8,128)(2,1)S(1)} all-gather(bf16[1,184,128]{2,1,0:T(8,128)(2,1)S(1)} %fusion.30), channel_id=1, replica_groups=mesh['batch'=8,'owner'=4] {'batch'}, dimensions={0}, use_global_device_ids=true | all-gather | bytes 423936 | tf_op jit(solution)/shard_map/all_gather | solution.py:50
  44.8 10.7 %while.20 = (s32[]{:T(128)}, f32[2,8,6]{2,1,0:T(8,128)S(1)}, s32[2]{0:T(128)S(1)}, s32[16,6]{1,0:T(8,128)S(1)}, s32[16,6]{1,0:T(8,128)S(1)}, /*index=5*/bf16[8,1...) while((s32[]{:T(128)}, f32[2,8,6]{2,1,0:T(8,128)S(1)}, ...), condition=%wide.region_8.10_spmd, body=%wide.region_5.9_spmd.sunk | while | flops 74615640 | bytes 6876823 | solution.py:76
  44.8 0.7 dynamic_slice.51
  46.2 0.1 reshape.156
  46.2 1.0 gather_fusion
  47.3 2.5 %fusion.56 = f32[8,6,32]{2,1,0:T(8,128)S(1)} fusion(bf16[8,6,184,128]{3,2,1,0:T(8,128)(2,1)S(1)} %bitcast.65, pred[8,6]{1,0:T(8,128)(4,1)S(1)} %get-tuple-element.291, s32[8,6]{1,0:T(8,128)S(1)} %get-tuple-element.292, bf16[16,32,128]{2,1,0:T(8,128)(2,1)} %get-tuple-element.332, s32[]{:T(128)S(6)} %select_n.129), kind=kOutput, calls=%fused_computation.8.clone.1 | convolution fusion | flops 74611200 | bytes 2332916 | tf_op jit(solution)/shard_map/while/body/eval_jaxpr/bid,bktd->bkit/dot_general | solution.py:21
  49.8 0.2 log_reduce_fusion.2
  49.9 0.1 copy.63
  50.0 0.1 copy.64
  50.1 0.7 dynamic_slice.51
  51.5 0.1 reshape.156
  51.6 1.0 gather_fusion
  52.6 2.5 %fusion.56 = f32[8,6,32]{2,1,0:T(8,128)S(1)} fusion(bf16[8,6,184,128]{3,2,1,0:T(8,128)(2,1)S(1)} %bitcast.65, pred[8,6]{1,0:T(8,128)(4,1)S(1)} %get-tuple-element.291, s32[8,6]{1,0:T(8,128)S(1)} %get-tuple-element.292, bf16[16,32,128]{2,1,0:T(8,128)(2,1)} %get-tuple-element.332, s32[]{:T(128)S(6)} %select_n.129), kind=kOutput, calls=%fused_computation.8.clone.1 | convolution fusion | flops 74611200 | bytes 2332916 | tf_op jit(solution)/shard_map/while/body/eval_jaxpr/bid,bktd->bkit/dot_general | solution.py:21
  55.1 0.2 log_reduce_fusion.2
  55.3 0.1 copy.63
  55.4 0.1 copy.64
  55.5 0.1 copy.55
  55.6 0.1 select_reduce_fusion.1
  55.7 5.8 %all-reduce = f32[16,12]{1,0:T(8,128)S(1)} all-reduce(f32[16,12]{1,0:T(8,128)S(1)} %select_reduce_fusion.1), channel_id=2, replica_groups=mesh['batch'=8,'owner'=4] {'owner'}, use_global_device_ids=true, to_apply=%region_10.12.clone | all-reduce | flops 192 | bytes 1536
  61.4 0.6 dynamic-slice
  62.7 0.1 exponential_reduce_fusion.1
  62.8 0.1 exponential_reduce_fusion
  63.0 0.7 multiply_reduce_fusion
  63.7 5.2 %all-gather = f32[4,4,12]{2,1,0:T(4,128)S(1)} all-gather(f32[1,4,12]{2,1,0:T(4,128)S(1)} %get-tuple-element.199), channel_id=1, replica_groups=mesh['batch'=8,'owner'=4] {'owner'}, dimensions={0}, use_global_device_ids=true | all-gather | bytes 960 | tf_op jit(solution)/shard_map/all_gather | solution.py:80
  68.8 0.1 select_reduce_fusion
  68.9 22.7 %while.21 = (s32[]{:T(128)}, f32[2,8,32,128]{3,2,1,0:T(8,128)}, s32[2]{0:T(128)S(1)}, f32[16,6]{0,1:T(8,128)S(1)}, s32[16,6]{1,0:T(8,128)S(1)}, /*index=5*/s32[1...) while((s32[]{:T(128)}, f32[2,8,32,128]{3,2,1,0:T(8,128)}, ...), condition=%wide.region_16.18_spmd, body=%wide.region_14.17_spmd.sunk | while | flops 150739936 | bytes 13344207 | solution.py:95
  69.0 0.7 dynamic_slice.55
  70.3 0.1 reshape.159
  70.4 1.0 gather_fusion.1
  71.5 3.5 %bitcast_select_fusion.3 = f32[8,6,32,184]{3,2,1,0:T(8,128)} fusion(bf16[8,6,184,128]{3,2,1,0:T(8,128)(2,1)S(1)} %bitcast.66, pred[8,6]{1,0:T(8,128)(4,1)S(1)} %get-tuple-element.303, s32[8,6]{1,0:T(8,128)S(1)} %constant_dynamic-slice_fusion.4, bf16[16,32,128]{2,1,0:T(8,128)(2,1)} %get-tuple-element.368, s32[]{:T(128)S(6)} %select_n.133), kind=kOutput, calls=%fused_computation.25.clone.1 | convolution fusion | flops 74330112 | bytes 3457268 | tf_op jit(solution)/shard_map/while/body/eval_jaxpr/bid,bktd->bkit/dot_general | solution.py:21
  75.0 3.0 %fusion.61 = f32[8,6,32,128]{3,2,1,0:T(8,128)S(1)} fusion(bf16[8,6,184,128]{3,2,1,0:T(8,128)(2,1)S(1)} %bitcast.67, pred[8,6]{1,0:T(8,128)(4,1)S(1)} %get-tuple-element.303, f32[8,6,32,184]{3,2,1,0:T(8,128)} %bitcast_select_fusion.3), kind=kOutput, calls=%fused_computation.23.clone.1 | convolution fusion | flops 74049208 | bytes 4177968 | tf_op jit(solution)/shard_map/while/body/eval_jaxpr/bkit,bktd->bkid/dot_general | solution.py:91
  78.1 0.1 dynamic-slice_bitcast_fusion.2
  78.2 0.1 copy.66
  78.2 1.4 %fusion.62 = f32[8,1,32,128]{3,1,2,0:T(1,128)S(1)} fusion(f32[8,6,1,1]{1,2,3,0:T(1,128)S(1)} %copy.66, f32[8,6,32,128]{3,2,1,0:T(8,128)S(1)} %fusion.61), kind=kOutput, calls=%fused_computation.30.clone.1 | convolution fusion | flops 2359296 | bytes 917696 | tf_op jit(solution)/shard_map/while/body/eval_jaxpr/bk,bkid->bid/dot_general | solution.py:92
  79.6 0.7 constant_dynamic-update-slice_fusion.2
  80.3 0.7 dynamic_slice.55
  81.7 0.1 reshape.159
  81.8 1.0 gather_fusion.1
  82.8 3.5 %bitcast_select_fusion.3 = f32[8,6,32,184]{3,2,1,0:T(8,128)} fusion(bf16[8,6,184,128]{3,2,1,0:T(8,128)(2,1)S(1)} %bitcast.66, pred[8,6]{1,0:T(8,128)(4,1)S(1)} %get-tuple-element.303, s32[8,6]{1,0:T(8,128)S(1)} %constant_dynamic-slice_fusion.4, bf16[16,32,128]{2,1,0:T(8,128)(2,1)} %get-tuple-element.368, s32[]{:T(128)S(6)} %select_n.133), kind=kOutput, calls=%fused_computation.25.clone.1 | convolution fusion | flops 74330112 | bytes 3457268 | tf_op jit(solution)/shard_map/while/body/eval_jaxpr/bid,bktd->bkit/dot_general | solution.py:21
  86.4 3.0 %fusion.61 = f32[8,6,32,128]{3,2,1,0:T(8,128)S(1)} fusion(bf16[8,6,184,128]{3,2,1,0:T(8,128)(2,1)S(1)} %bitcast.67, pred[8,6]{1,0:T(8,128)(4,1)S(1)} %get-tuple-element.303, f32[8,6,32,184]{3,2,1,0:T(8,128)} %bitcast_select_fusion.3), kind=kOutput, calls=%fused_computation.23.clone.1 | convolution fusion | flops 74049208 | bytes 4177968 | tf_op jit(solution)/shard_map/while/body/eval_jaxpr/bkit,bktd->bkid/dot_general | solution.py:91
  89.5 0.1 copy.66
  89.6 1.4 %fusion.62 = f32[8,1,32,128]{3,1,2,0:T(1,128)S(1)} fusion(f32[8,6,1,1]{1,2,3,0:T(1,128)S(1)} %copy.66, f32[8,6,32,128]{3,2,1,0:T(8,128)S(1)} %fusion.61), kind=kOutput, calls=%fused_computation.30.clone.1 | convolution fusion | flops 2359296 | bytes 917696 | tf_op jit(solution)/shard_map/while/body/eval_jaxpr/bk,bkid->bid/dot_general | solution.py:92
  91.0 0.7 constant_dynamic-update-slice_fusion.2
  91.7 9.4 %all_to_all.5 = f32[4,4,32,128]{3,2,1,0:T(8,128)S(1)} all-to-all(f32[4,4,32,128]{3,2,1,0:T(8,128)} %bitcast.69), channel_id=1, replica_groups=mesh['batch'=8,'owner'=4] {'owner'}, dimensions={0} | all-to-all | bytes 524288 | tf_op jit(solution)/shard_map/all_to_all | solution.py:99
  101.1 1.1 %fusion.28 = f32[4,32,128]{2,1,0:T(8,128)} fusion(f32[4,32,128]{2,1,0:T(8,128)S(1)} %reduce_sum.127, bf16[4,32,128]{2,1,0:T(8,128)(2,1)S(1)} %copy-done.2, f32[4,32]{1,0:T(4,128)S(1)} %add_rsqrt_fusion), kind=kOutput, calls=%fused_computation.48 | output fusion | flops 131327 | bytes 164352 | tf_op jit(solution)/shard_map/mul | solution.py:102
  (46 shorter events, 0.4 us)
Async XLA Ops:
  0.6 0.8 copy-start
  1.5 1.7 %copy-start.4 = (s32[16,12]{1,0:T(8,128)S(1)}, s32[16,12]{1,0:T(8,128)}, u32[]{:S(2)}) copy-start(s32[16,12]{1,0:T(8,128)} %param.15) | copy-start | bytes 2308
  3.0 1.0 copy-start.1
  4.0 1.5 %copy-start.2 = (bf16[4,32,128]{2,1,0:T(8,128)(2,1)S(1)}, bf16[4,32,128]{2,1,0:T(8,128)(2,1)}, u32[]{:S(2)}) copy-start(bf16[4,32,128]{2,1,0:T(8,128)(2,1)} %param.12) | copy-start | bytes 98308
  4.0 8.7 %copy-start.3 = (bf16[1,184,128]{2,1,0:T(8,128)(2,1)S(1)}, bf16[1,184,128]{2,1,0:T(8,128)(2,1)}, u32[]{:S(2)}) copy-start(bf16[1,184,128]{2,1,0:T(8,128)(2,1)} %param.13) | copy-start | bytes 141316
  44.8 16.7 %copy-start.6 = (u32[32]{0:T(128)S(1)}, u32[32]{0:T(128)}, u32[]{:S(2)}) copy-start(u32[32]{0:T(128)} %constant.111) | copy-start | bytes 388
  44.8 18.1 %copy-start.5 = (f32[4,12]{1,0:T(4,128)S(1)}, f32[4,12]{1,0:T(4,128)}, u32[]{:S(2)}) copy-start(f32[4,12]{1,0:T(4,128)} %param.17) | copy-start | bytes 580
where the time goes:
time: 103 us; the launch traced here: 102 us
  blocking collectives  59.1 us (57%)
  matrix products  21 us (20%)
  local copies, waits for them, and re-layouts  13.2 us (13%)
  other arithmetic  4.46 us (4%)
  loops' own time  2.94 us (3%)
  between operations  1.51 us (1%)
    all_gather x1, blocking collectives, local(): cached = lax.all_gather(shard_unit, 'batch', axis=0, tiled=True)  31.8 us
    dot_general x4, matrix products, token_terms(): jnp.einsum('bid,bktd->bkit', query_block, passages, preferred_element_typ...  12.1 us
    all_to_all x1, blocking collectives, local(): lax.all_to_all(partials, 'owner', split_axis=0, concat_axis=0, tiled=True)  9.38 us
    all_gather x1, blocking collectives, local(): gathered = lax.all_gather(sent_query, 'owner', axis=0, tiled=True)  6.99 us
    dot_general x2, matrix products, one_block(): jnp.einsum('bkit,bktd->bkid', weights, passages, preferred_element_type=j...  6.09 us
    unnamed x1, blocking collectives  5.77 us
    all_gather x1, blocking collectives, local(): grad_rows = lax.all_gather(grad_own, 'owner', axis=0, tiled=True)  5.18 us
    gather x4, local copies, waits for them, and re-layouts, block_inputs(): return (query_block, jnp.take(cached, pick_block, axis=0), length_block)  4.05 us

commit v1 on v0

--- a/solution.py
+++ b/solution.py
@@ -9,6 +9,27 @@
 STUDENT_GAIN = 2.0
 LOSS_SCALE = 64.0
 EPSILON = 1e-06
+
+
+def post_flows(incoming_x, pos_dim):
+    upper = list(incoming_x.shape[1:])
+    upper[pos_dim] *= incoming_x.shape[0]
+    return jnp.moveaxis(incoming_x, 0, pos_dim).reshape(upper)
+
+
+def _supply_numbers(payload, lane_axis):
+    u1 = lax.axis_size(lane_axis)
+    frame_out = lax.axis_index(lane_axis)
+    extra, arr_next = (u1, frame_out)
+    g_now, fresh = (payload[None], 1)
+    while fresh < extra:
+        plain = lax.ppermute(g_now, lane_axis, [(it, it ^ fresh) for it in range(extra)])
+        z_new = arr_next & fresh == 0
+        mat_out = jnp.where(z_new, g_now, plain)
+        w_next = jnp.where(z_new, plain, g_now)
+        g_now = jnp.concatenate([mat_out, w_next])
+        fresh *= 2
+    return g_now
 
 
 def unit_rows(values):
@@ -47,7 +68,8 @@
     sent_query = unit_query.astype(jnp.bfloat16)
     gathered = lax.all_gather(sent_query, "owner", axis=0, tiled=True)
     shard_unit = unit_rows(pool)[0].astype(jnp.bfloat16)
-    cached = lax.all_gather(shard_unit, "batch", axis=0, tiled=True)
+    reached = _supply_numbers(shard_unit, "batch")
+    cached = post_flows(reached, 0)
     group_rows = cached.shape[0]
     slot_ids = jnp.take(owner_map, candidates, axis=0)
     local_slot = slot_ids - my_group * group_rows

time: 103 us -> 82.3 us (0.80)
  blocking collectives: 59.1 us -> 26.3 us
  starting transfers between devices: 0 us -> 7.33 us
  waiting for transfers between devices: 0 us -> 2.92 us
  other arithmetic: 4.46 us -> 6.25 us
    all_gather x1 -> x0, blocking collectives: 31.8 us -> none  [local(): cached = lax.all_gather(shard_unit, 'batch', axis=0, tiled=True)]
    ppermute x0 -> x3, starting transfers between devices: none -> 7.33 us  [_supply_numbers(): lax.ppermute(g_now, lane_axis, [(it, it ^ fresh) for it in range(extra)])]
    ppermute x0 -> x3, waiting for transfers between devices: none -> 2.92 us  [_supply_numbers(): lax.ppermute(g_now, lane_axis, [(it, it ^ fresh) for it in range(extra)])]
    all_gather x1, blocking collectives: 6.99 us -> 5.87 us  [local(): gathered = lax.all_gather(sent_query, 'owner', axis=0, tiled=True)]
  transfers between devices with their start and end apart: 0 -> 3, of which waited for: 0 -> 2; matrix products, arithmetic and copies ran while one was open for 0% -> 7% of each run, Pallas kernels for 0% -> 0%
where the time goes in v1:
time: 82.3 us; the launch traced here: 81.6 us
  blocking collectives  26.3 us (32%)
  matrix products  21 us (26%)
  local copies, waits for them, and re-layouts  13.3 us (16%)
  starting transfers between devices  7.33 us (9%)
  other arithmetic  6.25 us (8%)
  loops' own time  2.94 us (4%)
  waiting for transfers between devices  2.92 us (4%)
  between operations  1.61 us (2%)
    dot_general x4, matrix products, token_terms(): jnp.einsum('bid,bktd->bkit', query_block, passages, preferred_element_typ...  12.1 us
    all_to_all x1, blocking collectives, local(): lax.all_to_all(partials, 'owner', split_axis=0, concat_axis=0, tiled=True)  9.38 us
    ppermute x3, starting transfers between devices, _supply_numbers(): lax.ppermute(g_now, lane_axis, [(it, it ^ fresh) for it in range(extra)])  7.33 us
    dot_general x2, matrix products, one_block(): jnp.einsum('bkit,bktd->bkid', weights, passages, preferred_element_type=j...  6.09 us
    unnamed x1, blocking collectives  5.89 us
    all_gather x1, blocking collectives, local(): gathered = lax.all_gather(sent_query, 'owner', axis=0, tiled=True)  5.87 us
    all_gather x1, blocking collectives, local(): grad_rows = lax.all_gather(grad_own, 'owner', axis=0, tiled=True)  5.18 us
    gather x4, local copies, waits for them, and re-layouts, block_inputs(): return (query_block, jnp.take(cached, pick_block, axis=0), length_block)  4.05 us
  transfers between devices with their start and end apart: 3, of which 2 were waited for; matrix products, arithmetic and copies ran while one was open for 7% of the time, Pallas kernels for 0%

profile of v1, /device:TPU:0, one launch (start us, length us, event | category | flops | bytes accessed | tf_op | source)
XLA Modules:
  0.0 81.6 jit_solution(7939013639975664999)
XLA Ops:
  0.6 0.9 %fusion.29 = f32[184]{0:T(256)S(1)} fusion(bf16[1,184,128]{2,1,0:T(8,128)(2,1)} %param.13), kind=kLoop, calls=%fused_computation.55 | loop fusion | flops 70472 | bytes 47840 | tf_op jit(solution)/shard_map/reduce_sum | solution.py:37
  1.6 0.9 %fusion.38 = bf16[1,1,184,128]{3,2,0,1:T(8,128)(2,1)S(1)} fusion(bf16[1,184,128]{2,1,0:T(8,128)(2,1)} %param.13, f32[184]{0:T(256)S(1)} %add_rsqrt_fusion.1), kind=kLoop, calls=%fused_computation.72 | loop fusion | flops 70656 | bytes 94944 | tf_op jit(solution)/shard_map/broadcast_in_dim | solution.py:24
  2.5 3.0 %collective-permute-start = (bf16[1,1,184,128]{3,2,0,1:T(8,128)(2,1)S(1)}, bf16[1,1,184,128]{3,2,0,1:T(8,128)(2,1)S(1)}, u32[]{:S(2)}, u32[]{:S(2)}) collective-permute-start(bf16[1,1,184,128]{3,2,0,1:T(8,128)(2,1)S(1)} %fusion.38), channel_id=1, source_target_pairs={{0,4},{4,0},{8,12},{12,8},{16,20},{20,16},{24,28},{28,24},{1,5},{5... | collective-permute-start | bytes 141320 | tf_op jit(solution)/shard_map/ppermute | solution.py:26
  5.5 0.7 compare_select_fusion.2
  6.2 0.1 reshape.116
  6.3 1.6 %gather_fusion.2 = s32[192]{0:T(256)S(1)} fusion(s32[32]{0:T(128)S(1)} %copy-done, s32[1024]{0:T(1024)S(1)} %pad_clamp_fusion.3), kind=kCustom, calls=%fused_computation.2 | custom fusion | bytes 2304 | tf_op jit(solution)/shard_map/jit(_take)/gather | solution.py:74
  7.9 0.1 reshape.115
  8.0 0.2 reduce_window_sum.11
  8.2 0.2 fusion.37
  8.4 0.2 select_reduce_fusion.2
  8.6 0.1 copy.43
  8.6 0.1 reshape.124
  8.8 1.2 %gather_fusion.3 = s32[96]{0:T(128)S(1)} fusion(s32[8]{0:T(128)S(1)} %copy-done.1, s32[1024]{0:T(1024)S(1)} %pad_clamp_fusion.2), kind=kCustom, calls=%fused_computation.3 | custom fusion | bytes 1152 | tf_op jit(solution)/shard_map/jit(_take)/gather | solution.py:82
  10.0 0.1 reshape.123
  10.1 0.1 copy.44
  10.2 0.1 fusion.35
  10.3 0.1 copy.46
  10.4 0.1 copy.45
  10.5 0.1 broadcast_select_fusion.10
  10.6 1.6 %collective-permute-start.1 = (bf16[2,1,184,128]{3,2,0,1:T(8,128)(2,1)S(1)}, bf16[2,1,184,128]{3,2,0,1:T(8,128)(2,1)S(1)}, u32[]{:S(2)}, u32[]{:S(2)}) collective-permute-start(bf16[2,1,184,128]{3,2,0,1:T(8,128)(2,1)S(1)} %pad_maximum_fusion.1), channel_id=1, source_target_pairs={{0,8},{4,12},{8,0},{12,4},{16,24},{20,28},{24,16},{28,20},{1,9},{5... | collective-permute-start | bytes 282632 | tf_op jit(solution)/shard_map/ppermute | solution.py:26
  12.3 0.1 exponential_reduce_fusion
  12.4 0.7 dynamic-slice
  13.8 1.5 %collective-permute-done.1 = bf16[2,1,184,128]{3,2,0,1:T(8,128)(2,1)S(1)} collective-permute-done((bf16[2,1,184,128]{3,2,0,1:T(8,128)(2,1)S(1)}, bf16[2,1,184,128]{3,2,0,1:T(8,128)(2,1)S(1)}, u32[]{:S(2)}, u32[]{:S(2)}) %collective-permute-start.1) | collective-permute-done | bytes 94240 | tf_op jit(solution)/shard_map/ppermute | solution.py:26
  15.3 2.7 %collective-permute-start.2 = (bf16[4,1,184,128]{3,2,0,1:T(8,128)(2,1)S(1)}, bf16[4,1,184,128]{3,2,0,1:T(8,128)(2,1)S(1)}, u32[]{:S(2)}, u32[]{:S(2)}) collective-permute-start(bf16[4,1,184,128]{3,2,0,1:T(8,128)(2,1)S(1)} %pad_maximum_fusion), channel_id=1, source_target_pairs={{0,16},{4,20},{8,24},{12,28},{16,0},{20,4},{24,8},{28,12},{1,17},{... | collective-permute-start | bytes 565256 | tf_op jit(solution)/shard_map/ppermute | solution.py:26
  18.1 5.9 %all_gather.6 = bf16[16,32,128]{2,1,0:T(8,128)(2,1)} all-gather(bf16[4,32,128]{2,1,0:T(8,128)(2,1)S(1)} %fusion.32), channel_id=1, replica_groups=mesh['batch'=8,'owner'=4] {'owner'}, dimensions={0}, use_global_device_ids=true | all-gather | bytes 163840 | tf_op jit(solution)/shard_map/all_gather | solution.py:69
  23.9 1.4 %collective-permute-done.2 = bf16[4,1,184,128]{3,2,0,1:T(8,128)(2,1)S(1)} collective-permute-done((bf16[4,1,184,128]{3,2,0,1:T(8,128)(2,1)S(1)}, bf16[4,1,184,128]{3,2,0,1:T(8,128)(2,1)S(1)}, u32[]{:S(2)}, u32[]{:S(2)}) %collective-permute-start.2) | collective-permute-done | bytes 188448 | tf_op jit(solution)/shard_map/ppermute | solution.py:26
  25.5 10.7 %while.20 = (s32[]{:T(128)}, f32[2,8,6]{2,1,0:T(8,128)S(1)}, s32[2]{0:T(128)S(1)}, s32[16,6]{1,0:T(8,128)S(1)}, s32[16,6]{1,0:T(8,128)S(1)}, /*index=5*/bf16[8,1...) while((s32[]{:T(128)}, f32[2,8,6]{2,1,0:T(8,128)S(1)}, ...), condition=%wide.region_8.10_spmd, body=%wide.region_5.9_spmd.sunk | while | flops 74615640 | bytes 6876823 | solution.py:98
  25.5 0.7 dynamic_slice.51
  26.9 1.0 %gather_fusion = bf16[48,184,128]{2,1,0:T(8,128)(2,1)S(1)} fusion(bf16[8,184,128]{2,1,0:T(8,128)(2,1)S(1)} %get-tuple-element.337, s32[1024]{0:T(1024)S(1)} %pad_clamp_fusion.6), kind=kCustom, calls=%fused_computation.clone.clone.1 | custom fusion | bytes 4522176 | tf_op jit(solution)/shard_map/while/body/eval_jaxpr/jit(_take)/gather | solution.py:88
  28.0 2.5 %fusion.57 = f32[8,6,32]{2,1,0:T(8,128)S(1)} fusion(bf16[8,6,184,128]{3,2,1,0:T(8,128)(2,1)S(1)} %bitcast.71, pred[8,6]{1,0:T(8,128)(4,1)S(1)} %get-tuple-element.297, s32[8,6]{1,0:T(8,128)S(1)} %get-tuple-element.298, bf16[16,32,128]{2,1,0:T(8,128)(2,1)} %get-tuple-element.338, s32[]{:T(128)S(6)} %select_n.186), kind=kOutput, calls=%fused_computation.8.clone.1 | convolution fusion | flops 74611200 | bytes 2332916 | tf_op jit(solution)/shard_map/while/body/eval_jaxpr/bid,bktd->bkit/dot_general | solution.py:42
  30.5 0.2 log_reduce_fusion.2
  30.6 0.1 copy.63
  30.7 0.1 copy.64
  30.8 0.7 dynamic_slice.51
  32.2 0.1 reshape.160
  32.3 1.0 %gather_fusion = bf16[48,184,128]{2,1,0:T(8,128)(2,1)S(1)} fusion(bf16[8,184,128]{2,1,0:T(8,128)(2,1)S(1)} %get-tuple-element.337, s32[1024]{0:T(1024)S(1)} %pad_clamp_fusion.6), kind=kCustom, calls=%fused_computation.clone.clone.1 | custom fusion | bytes 4522176 | tf_op jit(solution)/shard_map/while/body/eval_jaxpr/jit(_take)/gather | solution.py:88
  33.3 2.5 %fusion.57 = f32[8,6,32]{2,1,0:T(8,128)S(1)} fusion(bf16[8,6,184,128]{3,2,1,0:T(8,128)(2,1)S(1)} %bitcast.71, pred[8,6]{1,0:T(8,128)(4,1)S(1)} %get-tuple-element.297, s32[8,6]{1,0:T(8,128)S(1)} %get-tuple-element.298, bf16[16,32,128]{2,1,0:T(8,128)(2,1)} %get-tuple-element.338, s32[]{:T(128)S(6)} %select_n.186), kind=kOutput, calls=%fused_computation.8.clone.1 | convolution fusion | flops 74611200 | bytes 2332916 | tf_op jit(solution)/shard_map/while/body/eval_jaxpr/bid,bktd->bkit/dot_general | solution.py:42
  35.8 0.2 log_reduce_fusion.2
  36.0 0.1 copy.63
  36.1 0.1 copy.64
  36.2 0.1 copy.55
  36.3 0.1 select_reduce_fusion.1
  36.4 5.9 %all-reduce = f32[16,12]{1,0:T(8,128)S(1)} all-reduce(f32[16,12]{1,0:T(8,128)S(1)} %select_reduce_fusion.1), channel_id=2, replica_groups=mesh['batch'=8,'owner'=4] {'owner'}, use_global_device_ids=true, to_apply=%region_10.12.clone | all-reduce | flops 192 | bytes 1536
  42.2 0.1 exponential_reduce_fusion.1
  42.4 0.7 multiply_reduce_fusion
  43.1 5.2 %all-gather = f32[4,4,12]{2,1,0:T(4,128)S(1)} all-gather(f32[1,4,12]{2,1,0:T(4,128)S(1)} %get-tuple-element.205), channel_id=1, replica_groups=mesh['batch'=8,'owner'=4] {'owner'}, dimensions={0}, use_global_device_ids=true | all-gather | bytes 960 | tf_op jit(solution)/shard_map/all_gather | solution.py:102
  48.3 0.1 select_reduce_fusion
  48.4 22.7 %while.21 = (s32[]{:T(128)}, f32[2,8,32,128]{3,2,1,0:T(8,128)}, s32[2]{0:T(128)S(1)}, f32[16,6]{0,1:T(8,128)S(1)}, s32[16,6]{1,0:T(8,128)S(1)}, /*index=5*/s32[1...) while((s32[]{:T(128)}, f32[2,8,32,128]{3,2,1,0:T(8,128)}, ...), condition=%wide.region_16.18_spmd, body=%wide.region_14.17_spmd.sunk | while | flops 150739936 | bytes 13344207 | solution.py:117
  48.4 0.7 dynamic_slice.55
  49.9 1.0 %gather_fusion.1 = bf16[48,184,128]{2,1,0:T(8,128)(2,1)S(1)} fusion(bf16[8,184,128]{2,1,0:T(8,128)(2,1)S(1)} %get-tuple-element.373, s32[1024]{0:T(1024)S(1)} %pad_clamp_fusion.7), kind=kCustom, calls=%fused_computation.1.clone.clone.1 | custom fusion | bytes 4522176 | tf_op jit(solution)/shard_map/while/body/eval_jaxpr/jit(_take)/gather | solution.py:88
  50.9 3.5 %bitcast_select_fusion.3 = f32[8,6,32,184]{3,2,1,0:T(8,128)} fusion(bf16[8,6,184,128]{3,2,1,0:T(8,128)(2,1)S(1)} %bitcast.72, pred[8,6]{1,0:T(8,128)(4,1)S(1)} %get-tuple-element.309, s32[8,6]{1,0:T(8,128)S(1)} %constant_dynamic-slice_fusion.4, bf16[16,32,128]{2,1,0:T(8,128)(2,1)} %get-tuple-element.374, s32[]{:T(128)S(6)} %select_n.190), kind=kOutput, calls=%fused_computation.25.clone.1 | convolution fusion | flops 74330112 | bytes 3457268 | tf_op jit(solution)/shard_map/while/body/eval_jaxpr/bid,bktd->bkit/dot_general | solution.py:42
  54.4 3.0 %fusion.62 = f32[8,6,32,128]{3,2,1,0:T(8,128)S(1)} fusion(bf16[8,6,184,128]{3,2,1,0:T(8,128)(2,1)S(1)} %bitcast.73, pred[8,6]{1,0:T(8,128)(4,1)S(1)} %get-tuple-element.309, f32[8,6,32,184]{3,2,1,0:T(8,128)} %bitcast_select_fusion.3), kind=kOutput, calls=%fused_computation.23.clone.1 | convolution fusion | flops 74049208 | bytes 4177968 | tf_op jit(solution)/shard_map/while/body/eval_jaxpr/bkit,bktd->bkid/dot_general | solution.py:113
  57.6 0.1 copy.66
  57.7 1.4 %fusion.63 = f32[8,1,32,128]{3,1,2,0:T(1,128)S(1)} fusion(f32[8,6,1,1]{1,2,3,0:T(1,128)S(1)} %copy.66, f32[8,6,32,128]{3,2,1,0:T(8,128)S(1)} %fusion.62), kind=kOutput, calls=%fused_computation.30.clone.1 | convolution fusion | flops 2359296 | bytes 917696 | tf_op jit(solution)/shard_map/while/body/eval_jaxpr/bk,bkid->bid/dot_general | solution.py:114
  59.1 0.7 constant_dynamic-update-slice_fusion.2
  59.7 0.7 dynamic_slice.55
  61.2 1.0 %gather_fusion.1 = bf16[48,184,128]{2,1,0:T(8,128)(2,1)S(1)} fusion(bf16[8,184,128]{2,1,0:T(8,128)(2,1)S(1)} %get-tuple-element.373, s32[1024]{0:T(1024)S(1)} %pad_clamp_fusion.7), kind=kCustom, calls=%fused_computation.1.clone.clone.1 | custom fusion | bytes 4522176 | tf_op jit(solution)/shard_map/while/body/eval_jaxpr/jit(_take)/gather | solution.py:88
  62.2 3.5 %bitcast_select_fusion.3 = f32[8,6,32,184]{3,2,1,0:T(8,128)} fusion(bf16[8,6,184,128]{3,2,1,0:T(8,128)(2,1)S(1)} %bitcast.72, pred[8,6]{1,0:T(8,128)(4,1)S(1)} %get-tuple-element.309, s32[8,6]{1,0:T(8,128)S(1)} %constant_dynamic-slice_fusion.4, bf16[16,32,128]{2,1,0:T(8,128)(2,1)} %get-tuple-element.374, s32[]{:T(128)S(6)} %select_n.190), kind=kOutput, calls=%fused_computation.25.clone.1 | convolution fusion | flops 74330112 | bytes 3457268 | tf_op jit(solution)/shard_map/while/body/eval_jaxpr/bid,bktd->bkit/dot_general | solution.py:42
  65.8 3.0 %fusion.62 = f32[8,6,32,128]{3,2,1,0:T(8,128)S(1)} fusion(bf16[8,6,184,128]{3,2,1,0:T(8,128)(2,1)S(1)} %bitcast.73, pred[8,6]{1,0:T(8,128)(4,1)S(1)} %get-tuple-element.309, f32[8,6,32,184]{3,2,1,0:T(8,128)} %bitcast_select_fusion.3), kind=kOutput, calls=%fused_computation.23.clone.1 | convolution fusion | flops 74049208 | bytes 4177968 | tf_op jit(solution)/shard_map/while/body/eval_jaxpr/bkit,bktd->bkid/dot_general | solution.py:113
  68.9 0.1 copy.66
  69.0 1.4 %fusion.63 = f32[8,1,32,128]{3,1,2,0:T(1,128)S(1)} fusion(f32[8,6,1,1]{1,2,3,0:T(1,128)S(1)} %copy.66, f32[8,6,32,128]{3,2,1,0:T(8,128)S(1)} %fusion.62), kind=kOutput, calls=%fused_computation.30.clone.1 | convolution fusion | flops 2359296 | bytes 917696 | tf_op jit(solution)/shard_map/while/body/eval_jaxpr/bk,bkid->bid/dot_general | solution.py:114
  70.4 0.7 constant_dynamic-update-slice_fusion.2
  71.1 9.4 %all_to_all.5 = f32[4,4,32,128]{3,2,1,0:T(8,128)S(1)} all-to-all(f32[4,4,32,128]{3,2,1,0:T(8,128)} %bitcast.75), channel_id=1, replica_groups=mesh['batch'=8,'owner'=4] {'owner'}, dimensions={0} | all-to-all | bytes 524288 | tf_op jit(solution)/shard_map/all_to_all | solution.py:121
  80.5 1.1 %fusion.28 = f32[4,32,128]{2,1,0:T(8,128)} fusion(f32[4,32,128]{2,1,0:T(8,128)S(1)} %reduce_sum.127, bf16[4,32,128]{2,1,0:T(8,128)(2,1)S(1)} %copy-done.3, f32[4,32]{1,0:T(4,128)S(1)} %add_rsqrt_fusion), kind=kOutput, calls=%fused_computation.48 | output fusion | flops 131327 | bytes 164352 | tf_op jit(solution)/shard_map/mul | solution.py:124
  (57 shorter events, 0.9 us)
Async XLA Ops:
  0.6 5.7 %copy-start = (s32[32]{0:T(128)S(1)}, s32[32]{0:T(128)}, u32[]{:S(2)}) copy-start(s32[32]{0:T(128)} %param.16) | copy-start | bytes 388
  2.5 8.1 %collective-permute-start = (bf16[1,1,184,128]{3,2,0,1:T(8,128)(2,1)S(1)}, bf16[1,1,184,128]{3,2,0,1:T(8,128)(2,1)S(1)}, u32[]{:S(2)}, u32[]{:S(2)}) collective-permute-start(bf16[1,1,184,128]{3,2,0,1:T(8,128)(2,1)S(1)} %fusion.38), channel_id=1, source_target_pairs={{0,4},{4,0},{8,12},{12,8},{16,20},{20,16},{24,28},{28,24},{1,5},{5... | collective-permute-start | bytes 141320 | tf_op jit(solution)/shard_map/ppermute | solution.py:26
  6.3 1.7 %copy-start.4 = (s32[16,12]{1,0:T(8,128)S(1)}, s32[16,12]{1,0:T(8,128)}, u32[]{:S(2)}) copy-start(s32[16,12]{1,0:T(8,128)} %param.15) | copy-start | bytes 2308
  7.9 0.9 %copy-start.1 = (s32[8]{0:T(128)S(1)}, s32[8]{0:T(128)}, u32[]{:S(2)}) copy-start(s32[8]{0:T(128)} %param.14) | copy-start | bytes 100
  8.8 1.4 %copy-start.3 = (bf16[4,32,128]{2,1,0:T(8,128)(2,1)S(1)}, bf16[4,32,128]{2,1,0:T(8,128)(2,1)}, u32[]{:S(2)}) copy-start(bf16[4,32,128]{2,1,0:T(8,128)(2,1)} %param.12) | copy-start | bytes 98308
  8.8 1.7 %copy-start.2 = (bf16[1,184,128]{2,1,0:T(8,128)(2,1)S(1)}, bf16[1,184,128]{2,1,0:T(8,128)(2,1)}, u32[]{:S(2)}) copy-start(bf16[1,184,128]{2,1,0:T(8,128)(2,1)} %param.13) | copy-start | bytes 141316
  8.8 3.5 %copy-start.5 = (f32[4,12]{1,0:T(4,128)S(1)}, f32[4,12]{1,0:T(4,128)}, u32[]{:S(2)}) copy-start(f32[4,12]{1,0:T(4,128)} %param.17) | copy-start | bytes 580
  8.8 3.6 %copy-start.6 = (u32[32]{0:T(128)S(1)}, u32[32]{0:T(128)}, u32[]{:S(2)}) copy-start(u32[32]{0:T(128)} %constant.120) | copy-start | bytes 388
  10.6 4.6 %collective-permute-start.1 = (bf16[2,1,184,128]{3,2,0,1:T(8,128)(2,1)S(1)}, bf16[2,1,184,128]{3,2,0,1:T(8,128)(2,1)S(1)}, u32[]{:S(2)}, u32[]{:S(2)}) collective-permute-start(bf16[2,1,184,128]{3,2,0,1:T(8,128)(2,1)S(1)} %pad_maximum_fusion.1), channel_id=1, source_target_pairs={{0,8},{4,12},{8,0},{12,4},{16,24},{20,28},{24,16},{28,20},{1,9},{5... | collective-permute-start | bytes 282632 | tf_op jit(solution)/shard_map/ppermute | solution.py:26
  15.3 10.0 %collective-permute-start.2 = (bf16[4,1,184,128]{3,2,0,1:T(8,128)(2,1)S(1)}, bf16[4,1,184,128]{3,2,0,1:T(8,128)(2,1)S(1)}, u32[]{:S(2)}, u32[]{:S(2)}) collective-permute-start(bf16[4,1,184,128]{3,2,0,1:T(8,128)(2,1)S(1)} %pad_maximum_fusion), channel_id=1, source_target_pairs={{0,16},{4,20},{8,24},{12,28},{16,0},{20,4},{24,8},{28,12},{1,17},{... | collective-permute-start | bytes 565256 | tf_op jit(solution)/shard_map/ppermute | solution.py:26
